TPU v7x, 512 devices: a whole 4x8x8 slice. The times are simulated.
512 devices in a mesh: chan: 8 (over z), tm: 64 (over x, y, core).
Axes of the slice: x: 4, y: 8, z: 8, core: 2. Of those that a mesh axis runs over, the one named last changes fastest.
Arguments:
- voltages: bfloat16 [8, 2, 128, 131072], P(None, None, 'chan', 'tm'), may hold values from -100 to 100
- prototype: float32 [64], replicated, may hold values from -5 to 5
- forget: float32 [8], P('chan'), may hold values from 0.5 to 16
Outputs:
- whitened: bfloat16 [8, 256, 131072], P('chan', None, 'tm')
All inputs are finite; a program needn't handle non-finite values.
Results may differ from a plain program's by a relative error of at most 0.0071.
Values may be sent and summed in bfloat16 or wider, within the bound.
No kernel may reach another device: no remote copies, remote signals or barrier semaphores. Data moves between devices by JAX's collectives and lax.ppermute only.
A program may use at most 64 MiB of HBM per device.

v0:
```python
import math
import jax
import jax.numpy as jnp
from jax import lax
from jax.sharding import PartitionSpec as P


def passed_along(value, axis, steps):
    count = lax.axis_size(axis)
    leading, last = (max(0, -steps), min(count, count - steps))
    return lax.ppermute(value, axis, [(source, source + steps) for source in range(leading, last)])


def carried_in(value, axis, join, neutral):
    count, mine = (lax.axis_size(axis), lax.axis_index(axis))
    pieces = jax.tree.map(lambda part: lax.all_gather(part, axis), value)
    total = jax.tree.map(
        lambda part, zero: jnp.full_like(part, 0) + jnp.asarray(zero, part.dtype), value, neutral
    )

    def hop(position, total):
        longer = join(total, jax.tree.map(lambda part: part[position], pieces))
        return jax.tree.map(lambda new, old: jnp.where(position < mine, new, old), longer, total)

    return lax.fori_loop(0, count - 1, hop, total)


def coefficient_table(prototype, tap_count, filter_branches):
    shaped = prototype.reshape(tap_count, filter_branches)
    steps_p = jnp.arange(filter_branches, dtype=jnp.float32)
    phase = 2.0 * math.pi / filter_branches * (steps_p[:, None] * steps_p[None, :])
    cosine = jnp.cos(phase)
    sine = jnp.sin(phase)
    pattern = jnp.stack([jnp.stack([cosine, -sine], -1), jnp.stack([sine, cosine], -1)], axis=1)
    return (shaped[:, :, None, None, None] * pattern[None]).astype(jnp.bfloat16)


def combine_stats(earlier, later):
    gram_e, count_e, retain_e = earlier
    gram_l, count_l, retain_l = later
    return (
        gram_e * retain_l[:, None, None] + gram_l,
        count_e * retain_l + count_l,
        retain_e * retain_l,
    )


def per_device(voltages, prototype, forget):
    filter_branches = voltages.shape[0]
    local_antenna_count = voltages.shape[2]
    frame_rows = voltages.shape[3]
    tap_count = prototype.shape[0] // filter_branches
    coef_table = coefficient_table(prototype, tap_count, filter_branches)
    tail_rows = passed_along(voltages[..., frame_rows - (tap_count - 1) :], "tm", 1)
    extended = jnp.concatenate([tail_rows, voltages], axis=3)
    branch_sum = jnp.zeros((filter_branches, local_antenna_count, 2, frame_rows), jnp.float32)
    for tap_idx in range(tap_count):
        branch_sum = branch_sum + jnp.einsum(
            "pcaf,pckq->kaqf",
            extended[..., tap_idx : tap_idx + frame_rows],
            coef_table[tap_idx],
            preferred_element_type=jnp.float32,
        )
    spectrum_rows = branch_sum.reshape(filter_branches, local_antenna_count * 2, frame_rows).astype(
        jnp.bfloat16
    )
    turned = lax.all_to_all(spectrum_rows, "chan", split_axis=0, concat_axis=1, tiled=True)
    channels_per_device = turned.shape[0]
    col_count = turned.shape[1]
    gram_now = jnp.einsum("cif,cjf->cij", turned, turned, preferred_element_type=jnp.float32)
    retain = jnp.exp(-forget / lax.axis_size("tm"))
    row_count = jnp.full((channels_per_device,), float(frame_rows), jnp.float32)
    zero_count = jnp.zeros((channels_per_device,), jnp.float32)
    unit_retain = jnp.ones((channels_per_device,), jnp.float32)
    prior_gram, prior_count, unused_retain = carried_in(
        (gram_now, row_count, retain),
        "tm",
        combine_stats,
        (jnp.zeros_like(gram_now), zero_count, unit_retain),
    )
    moment = retain[:, None, None] * prior_gram + gram_now
    weight_sum = retain * prior_count + jnp.float32(frame_rows)
    factor_low = jnp.linalg.cholesky(moment / weight_sum[:, None, None])
    identity_m = jnp.broadcast_to(jnp.eye(col_count, dtype=jnp.float32), factor_low.shape)
    inverse = lax.linalg.triangular_solve(factor_low, identity_m, left_side=True, lower=True)
    whitened = jnp.einsum(
        "cij,cjf->cif", inverse, turned.astype(jnp.float32), precision=lax.Precision.HIGHEST
    )
    return whitened.astype(jnp.bfloat16)


def solution(mesh):
    placed = (P(None, None, "chan", "tm"), P(), P("chan"))
    return jax.shard_map(
        per_device, mesh=mesh, in_specs=placed, out_specs=P("chan", None, "tm"), check_vma=False
    )
```

profile of v0, /device:TPU:1, one launch (start us, length us, event | category | flops | bytes accessed | tf_op | source)
XLA Modules:
  0.0 499.1 jit_solution(7681647442495996566)
XLA Ops:
  6.5 1.9 copy.32
  8.5 4.6 collective-permute-start
  14.7 2.7 collective-permute-done
  22.2 35.6 %all_to_all.4 = bf16[8,32,2048]{2,1,0:T(8,128)(2,1)S(1)} all-to-all(bf16[8,32,2048]{2,1,0:T(8,128)(2,1)S(1)} %copy.36), channel_id=1, replica_groups=mesh['chan'=8,'tm'=64] {'chan'}, dimensions={0} | all-to-all | bytes 2097152 | tf_op jit(solution)/shard_map/all_to_all | solution.py:67
  62.3 125.6 %all-reduce.3 = (f32[64]{0:T(128)S(1)}, f32[64]{0:T(128)S(1)}) all-reduce(f32[64]{0:T(128)S(1)} %fusion.66, f32[64]{0:T(128)S(1)} %dynamic-update-slice.12), channel_id=2, replica_groups=mesh['chan'=8,'tm'=64] {'tm'}, use_global_device_ids=true, to_apply=%add.1 | all-reduce | flops 128 | bytes 1024
  189.0 237.8 %while.18 = (s32[]{:T(128)}, f32[1,256,256]{2,1,0:T(8,128)S(1)}, f32[1]{0:T(128)}, s32[]{:T(128)}, f32[64,1]{0,1:T(1,128)S(1)}, /*index=5*/f32[64,1,256,256]{3,2...) while((s32[]{:T(128)}, f32[1,256,256]{2,1,0:T(8,128)S(1)}, f32[1]{0:T(128)}, s32[]{:T(128)}, ...), condition=%wide.region_1.2_spmd.clone, body=%wide.region_0.1_spmd.clone.sunk | while | flops 262151 | bytes 786610 | solution.py:25
  189.7 1.7 fusion.81
  193.5 1.7 fusion.81
  208.6 1.7 fusion.81
  235.0 1.7 fusion.81
  257.7 1.7 fusion.81
  280.3 1.7 fusion.81
  306.7 1.7 fusion.81
  329.4 1.7 fusion.81
  352.0 1.7 fusion.81
  378.4 1.7 fusion.81
  401.1 1.7 fusion.81
  423.7 1.7 fusion.81
  429.0 11.7 %custom-call.16 = f32[1,128,128]{2,1,0:T(8,128)S(1)} custom-call(f32[1,128,128]{2,1,0:T(8,128)S(1)} %cholesky.114), custom_call_target="Cholesky" | custom-call | tf_op jit(solution)/shard_map/jit(cholesky)/cholesky | solution.py:83
  440.8 9.8 %custom-call.17 = f32[1,1,128,128]{2,3,1,0:T(8,128)S(1)} custom-call(f32[1,1,128,128]{3,2,1,0:T(8,128)S(1)} %get-tuple-element.223), custom_call_target="InvertDiagBlocksLowerTriangular" | custom-call | tf_op jit(solution)/shard_map/jit(cholesky)/cholesky | solution.py:83
  451.1 11.7 %custom-call.18 = f32[1,128,128]{2,1,0:T(8,128)S(1)} custom-call(f32[1,128,128]{2,1,0:T(8,128)S(1)} %fusion.13), custom_call_target="Cholesky" | custom-call | tf_op jit(solution)/shard_map/jit(cholesky)/cholesky | solution.py:83
  465.6 4.0 while.17
  469.5 19.9 %custom-call.19 = f32[1,2,128,128]{2,3,1,0:T(8,128)S(1)} custom-call(f32[1,2,128,128]{3,2,1,0:T(8,128)S(1)} %bitcast.227), custom_call_target="InvertDiagBlocksLowerTriangular" | custom-call | tf_op jit(solution)/shard_map/triangular_solve | solution.py:85
  490.3 2.0 fusion.9
  (174 shorter events, 150.6 us)
Async XLA Ops:
  6.5 6.9 %copy-start = (bf16[8,2,16,2048]{3,2,1,0:T(8,128)(2,1)S(1)}, bf16[8,2,16,2048]{3,2,1,0:T(8,128)(2,1)}, u32[]{:S(2)}) copy-start(bf16[8,2,16,2048]{3,2,1,0:T(8,128)(2,1)} %param.5) | copy-start | bytes 3145732
  6.5 6.8 %copy-start.1 = (f32[64]{0:T(128)S(1)}, f32[64]{0:T(128)}, u32[]{:S(2)}) copy-start(f32[64]{0:T(128)} %param.6) | copy-start | bytes 772
  6.5 182.5 %all-gather.4.cloned.1.call-start = ((), (), s32[]{:S(2)}) async-start(), calls=%async_computation.1 | async-start | bytes 17039360 | tf_op jit(solution)/shard_map/all_gather | solution.py:16
  8.5 8.9 %collective-permute-start = (bf16[8,2,16,7]{3,0,1,2:T(8,128)(2,1)S(1)}, bf16[8,2,16,7]{3,0,1,2:T(8,128)(2,1)S(1)}, u32[]{:S(2)}, u32[]{:S(2)}) collective-permute-start(bf16[8,2,16,7]{3,0,1,2:T(8,128)(2,1)S(1)} %slice.121), channel_id=1, source_target_pairs={{0,1},{1,2},{2,3},{3,4},{4,5},{5,6},{6,7},{7,8},{8,9},{9,10},{10,1... | collective-permute-start | bytes 10760 | tf_op jit(solution)/shard_map/ppermute | solution.py:11
Sparse Core Ops, SparseCore 0:
  59.1 101.0 all-gather.3
where the time goes:
time: 507 us; the launch traced here: 499 us
  other arithmetic  167 us (33%)
  blocking collectives  161 us (32%)
  loops' own time  85.9 us (17%)
  local copies, waits for them, and re-layouts  52.1 us (10%)
  between operations  16.3 us (3%)
  matrix products  9.79 us (2%)
    unnamed x1, blocking collectives  126 us
    select_n x63, other arithmetic, hop(): jnp.where(position < mine, new, old)  110 us
    another operation x1, loops' own time, carried_in(): return lax.fori_loop(0, count - 1, hop, total)  85.8 us
    dynamic_slice x63, local copies, waits for them, and re-layouts, hop(): longer = join(total, jax.tree.map(lambda part: part[position], pieces))  42 us
    all_to_all x1, blocking collectives, per_device(): lax.all_to_all(spectrum_rows, 'chan', split_axis=0, concat_axis=1, tiled=...  35.6 us
    another operation x7, other arithmetic, per_device(): factor_low = jnp.linalg.cholesky(moment / weight_sum[:, None, None])  34.6 us
    another operation x3, other arithmetic, per_device(): lax.linalg.triangular_solve(factor_low, identity_m, left_side=True, lower...  19.9 us
  transfers between devices with their start and end apart: 2, of which 1 were waited for; matrix products, arithmetic and copies ran while one was open for 1% of the time, Pallas kernels for 0%

commit v1 on v0

--- a/solution.py
+++ b/solution.py
@@ -64,7 +64,10 @@
     spectrum_rows = branch_sum.reshape(filter_branches, local_antenna_count * 2, frame_rows).astype(
         jnp.bfloat16
     )
-    turned = lax.all_to_all(spectrum_rows, "chan", split_axis=0, concat_axis=1, tiled=True)
+    w2 = lax.all_to_all(
+        jnp.stack(jnp.split(spectrum_rows, lax.axis_size("chan"), axis=0), axis=0), "chan", 0, 0
+    )
+    turned = jnp.concatenate(w2, axis=1)
     channels_per_device = turned.shape[0]
     col_count = turned.shape[1]
     gram_now = jnp.einsum("cif,cjf->cij", turned, turned, preferred_element_type=jnp.float32)

time: 507 us -> 484 us (0.955)
  other arithmetic: 167 us -> 158 us
  loops' own time: 85.9 us -> 77 us
    another operation x1, loops' own time: 85.8 us -> 77 us  [carried_in(): return lax.fori_loop(0, count - 1, hop, total)]
    select_n x63, other arithmetic: 110 us -> 101 us  [hop(): jnp.where(position < mine, new, old)]
where the time goes in v1:
time: 484 us; the launch traced here: 480 us
  blocking collectives  161 us (33%)
  other arithmetic  158 us (33%)
  loops' own time  77 us (16%)
  local copies, waits for them, and re-layouts  50.5 us (10%)
  between operations  16.4 us (3%)
  matrix products  9.78 us (2%)
    unnamed x1, blocking collectives  125 us
    select_n x63, other arithmetic, hop(): jnp.where(position < mine, new, old)  101 us
    another operation x1, loops' own time, carried_in(): return lax.fori_loop(0, count - 1, hop, total)  77 us
    dynamic_slice x63, local copies, waits for them, and re-layouts, hop(): longer = join(total, jax.tree.map(lambda part: part[position], pieces))  37 us
    all_to_all x1, blocking collectives, per_device(): lax.all_to_all(jnp.stack(jnp.split(spectrum_rows, lax.axis_size('chan'),...  35.6 us
    another operation x7, other arithmetic, per_device(): factor_low = jnp.linalg.cholesky(moment / weight_sum[:, None, None])  34.6 us
    another operation x3, other arithmetic, per_device(): lax.linalg.triangular_solve(factor_low, identity_m, left_side=True, lower...  19.9 us
  transfers between devices with their start and end apart: 2, of which 1 were waited for; matrix products, arithmetic and copies ran while one was open for 1% of the time, Pallas kernels for 0%

profile of v1, /device:TPU:1, one launch (start us, length us, event | category | flops | bytes accessed | tf_op | source)
XLA Modules:
  0.0 479.8 jit_solution(10140956813355022432)
XLA Ops:
  6.5 1.9 copy.13
  8.5 4.6 collective-permute-start
  14.7 2.7 collective-permute-done
  21.5 1.8 fusion.69
  25.7 35.6 %all_to_all.5 = bf16[8,1,32,2048]{3,2,1,0:T(8,128)(2,1)S(1)} all-to-all(bf16[8,1,32,2048]{3,2,1,0:T(8,128)(2,1)S(1)} %constant_dynamic-update-slice_fusion), channel_id=1, replica_groups=mesh['chan'=8,'tm'=64] {'chan'}, dimensions={0} | all-to-all | bytes 2097152 | tf_op jit(solution)/shard_map/all_to_all | solution.py:67
  66.0 125.5 %all-reduce.3 = (f32[64]{0:T(128)S(1)}, f32[64]{0:T(128)S(1)}) all-reduce(f32[64]{0:T(128)S(1)} %fusion.66, f32[64]{0:T(128)S(1)} %dynamic-update-slice.12), channel_id=2, replica_groups=mesh['chan'=8,'tm'=64] {'tm'}, use_global_device_ids=true, to_apply=%add.1 | all-reduce | flops 128 | bytes 1024
  192.6 215.0 %while.18 = (s32[]{:T(128)}, f32[1,256,256]{2,1,0:T(8,128)S(1)}, f32[1]{0:T(128)}, s32[]{:T(128)}, f32[64,1]{0,1:T(1,128)S(1)}, /*index=5*/f32[64,1,256,256]{3,2...) while((s32[]{:T(128)}, f32[1,256,256]{2,1,0:T(8,128)S(1)}, f32[1]{0:T(128)}, s32[]{:T(128)}, ...), condition=%wide.region_1.2_spmd.clone, body=%wide.region_0.1_spmd.clone.sunk | while | flops 262151 | bytes 786610 | solution.py:25
  193.2 1.6 fusion.82
  196.7 1.6 fusion.82
  200.1 1.6 fusion.82
  203.5 1.6 fusion.82
  206.9 1.6 fusion.82
  210.3 1.6 fusion.82
  220.6 1.6 fusion.82
  224.0 1.6 fusion.82
  227.4 1.6 fusion.82
  230.8 1.6 fusion.82
  234.2 1.6 fusion.82
  409.9 11.7 %custom-call.16 = f32[1,128,128]{2,1,0:T(8,128)S(1)} custom-call(f32[1,128,128]{2,1,0:T(8,128)S(1)} %cholesky.114), custom_call_target="Cholesky" | custom-call | tf_op jit(solution)/shard_map/jit(cholesky)/cholesky | solution.py:86
  421.6 9.8 %custom-call.17 = f32[1,1,128,128]{2,3,1,0:T(8,128)S(1)} custom-call(f32[1,1,128,128]{3,2,1,0:T(8,128)S(1)} %get-tuple-element.217), custom_call_target="InvertDiagBlocksLowerTriangular" | custom-call | tf_op jit(solution)/shard_map/jit(cholesky)/cholesky | solution.py:86
  431.9 11.7 %custom-call.18 = f32[1,128,128]{2,1,0:T(8,128)S(1)} custom-call(f32[1,128,128]{2,1,0:T(8,128)S(1)} %fusion.13), custom_call_target="Cholesky" | custom-call | tf_op jit(solution)/shard_map/jit(cholesky)/cholesky | solution.py:86
  446.4 3.9 while.17
  450.3 19.9 %custom-call.19 = f32[1,2,128,128]{2,3,1,0:T(8,128)S(1)} custom-call(f32[1,2,128,128]{3,2,1,0:T(8,128)S(1)} %bitcast.225), custom_call_target="InvertDiagBlocksLowerTriangular" | custom-call | tf_op jit(solution)/shard_map/triangular_solve | solution.py:88
  471.0 2.0 fusion.9
  (197 shorter events, 141.7 us)
Async XLA Ops:
  6.5 6.9 %copy-start = (bf16[8,2,16,2048]{3,2,1,0:T(8,128)(2,1)S(1)}, bf16[8,2,16,2048]{3,2,1,0:T(8,128)(2,1)}, u32[]{:S(2)}) copy-start(bf16[8,2,16,2048]{3,2,1,0:T(8,128)(2,1)} %param.5) | copy-start | bytes 3145732
  6.5 6.8 %copy-start.1 = (f32[64]{0:T(128)S(1)}, f32[64]{0:T(128)}, u32[]{:S(2)}) copy-start(f32[64]{0:T(128)} %param.6) | copy-start | bytes 772
  6.5 186.1 %all-gather.4.cloned.1.call-start = ((), (), s32[]{:S(2)}) async-start(), calls=%async_computation.1 | async-start | bytes 17039360 | tf_op jit(solution)/shard_map/all_gather | solution.py:16
  8.5 8.9 %collective-permute-start = (bf16[8,2,16,7]{3,0,1,2:T(8,128)(2,1)S(1)}, bf16[8,2,16,7]{3,0,1,2:T(8,128)(2,1)S(1)}, u32[]{:S(2)}, u32[]{:S(2)}) collective-permute-start(bf16[8,2,16,7]{3,0,1,2:T(8,128)(2,1)S(1)} %slice.129), channel_id=1, source_target_pairs={{0,1},{1,2},{2,3},{3,4},{4,5},{5,6},{6,7},{7,8},{8,9},{9,10},{10,1... | collective-permute-start | bytes 10760 | tf_op jit(solution)/shard_map/ppermute | solution.py:11
Sparse Core Ops, SparseCore 0:
  62.5 100.9 all-gather.3
